TPU v7x, 32 devices: a whole 2x2x4 slice. The times are simulated.
32 devices in a mesh: dp: 4 (over y, x), seq: 8 (over z, core).
Axes of the slice: x: 2, y: 2, z: 4, core: 2. Of those that a mesh axis runs over, the one named last changes fastest.
Arguments:
- inputs: bfloat16 [8, 1024, 1280], P('dp', 'seq'), may hold values from -6 to 6
- cotangent: bfloat16 [8, 1024, 1280], P('dp', 'seq'), may hold values from -6 to 6
- w_query: bfloat16 [1280, 1280], P(('dp', 'seq')), may hold values from -0.15625 to 0.15625
- w_key: bfloat16 [1280, 1280], P(('dp', 'seq')), may hold values from -0.15625 to 0.15625
- w_value: bfloat16 [1280, 1280], P(('dp', 'seq')), may hold values from -0.15625 to 0.15625
- w_out: bfloat16 [1280, 1280], P(('dp', 'seq')), may hold values from -1.25 to 1.25
- w_up: bfloat16 [1280, 1280], P(('dp', 'seq')), may hold values from -0.15625 to 0.15625
- w_down: bfloat16 [1280, 1280], P(('dp', 'seq')), may hold values from -0.15625 to 0.15625
- norm_attn: bfloat16 [1280], P(('dp', 'seq')), may hold values from 0.5 to 1.5
- norm_mlp: bfloat16 [1280], P(('dp', 'seq')), may hold values from 0.5 to 1.5
- query_scale: bfloat16 [1280], P(('dp', 'seq')), may hold values from 0 to 1.5
Outputs:
- output: bfloat16 [8, 1024, 1280], P('dp', 'seq')
- input_grad: float32 [8, 1024, 1280], P('dp', 'seq')
- grad_query: float32 [1280, 1280], P(('dp', 'seq'))
- grad_key: float32 [1280, 1280], P(('dp', 'seq'))
- grad_value: float32 [1280, 1280], P(('dp', 'seq'))
- grad_out: float32 [1280, 1280], P(('dp', 'seq'))
- grad_up: float32 [1280, 1280], P(('dp', 'seq'))
- grad_down: float32 [1280, 1280], P(('dp', 'seq'))
- grad_norm_attn: float32 [1280], P(('dp', 'seq'))
- grad_norm_mlp: float32 [1280], P(('dp', 'seq'))
- grad_query_scale: float32 [1280], P(('dp', 'seq'))
All inputs are finite; a program needn't handle non-finite values.
Results may differ from a plain program's by a relative error of at most 0.014.
Values may be sent and summed in bfloat16 or wider, within the bound.
No kernel may reach another device: no remote copies, remote signals or barrier semaphores. Data moves between devices by JAX's collectives and lax.ppermute only.
A program may use at most 320 MiB of HBM per device.

v0:
```python
import math
import jax
import jax.numpy as jnp
from jax import lax
from jax.sharding import PartitionSpec as P

H = 16
EPS = 1e-06
SOFT_BASE = 1.442695


def weight_outer(left, right):
    return lax.dot_general(
        left, right, (((0,), (0,)), ((), ())), preferred_element_type=jnp.float32
    )


def times_transpose(left, right):
    return lax.dot_general(
        left, right, (((1,), (1,)), ((), ())), preferred_element_type=jnp.float32
    )


def norm_back(grad, normed, inverse, gain):
    scaled = grad * gain
    inner = jnp.mean(scaled * normed, axis=-1, keepdims=True)
    return (inverse * (scaled - normed * inner), jnp.sum(grad * normed, axis=0))


def attend(q_low, k_low, v_low, first_row, num_heads):
    group_rows, model_width = q_low.shape
    head_size = model_width // num_heads
    query_heads = q_low.reshape(group_rows, num_heads, head_size)
    query_place = first_row + lax.iota(jnp.int32, group_rows)
    start_state = (
        jnp.full((num_heads, group_rows), -1e30, jnp.float32),
        jnp.zeros((num_heads, group_rows), jnp.float32),
        jnp.zeros((group_rows, model_width), jnp.float32),
    )
    key_piece = lax.all_gather(k_low, "seq", axis=0, tiled=True)
    value_piece = lax.all_gather(v_low, "seq", axis=0, tiled=True)
    count = key_piece.shape[0]

    def attend_compute(state):
        best, total, accum = state
        key_heads = key_piece.reshape(count, num_heads, head_size)
        value_heads = value_piece.reshape(count, num_heads, head_size)
        scores = jnp.einsum(
            "qhd,khd->hqk", query_heads, key_heads, preferred_element_type=jnp.float32
        )
        key_place = lax.iota(jnp.int32, count)
        allowed = (key_place[None, :] <= query_place[:, None])[None]
        scores = jnp.where(allowed, scores, -1e30)
        fresh = jnp.maximum(best, jnp.max(scores, axis=2))
        shrink = jnp.exp(best - fresh)
        probs = jnp.where(allowed, jnp.exp(scores - fresh[:, :, None]), 0.0)
        total = jnp.sum(probs, axis=2)
        mixed = jnp.einsum(
            "hqk,khd->qhd",
            probs.astype(jnp.bfloat16),
            value_heads,
            preferred_element_type=jnp.float32,
        )
        factor = jnp.repeat(shrink.T, head_size, axis=1)
        return (fresh, total, accum * factor + mixed.reshape(group_rows, model_width))

    best, total, accum = lax.cond(
        jnp.int32(0) > first_row + group_rows - 1, lambda state: state, attend_compute, start_state
    )
    mixed = accum / jnp.repeat(total.T, head_size, axis=1)
    return (mixed, best + jnp.log(total))


def query_grads(q_low, d_mixed, k_low, v_low, log_total, row_delta, first_row, num_heads):
    group_rows, model_width = q_low.shape
    head_size = model_width // num_heads
    query_heads = q_low.reshape(group_rows, num_heads, head_size)
    grad_heads = d_mixed.reshape(group_rows, num_heads, head_size)
    query_place = first_row + lax.iota(jnp.int32, group_rows)
    empty = jnp.zeros((group_rows, model_width), jnp.float32)
    key_piece = lax.all_gather(k_low, "seq", axis=0, tiled=True)
    value_piece = lax.all_gather(v_low, "seq", axis=0, tiled=True)
    count = key_piece.shape[0]

    def query_compute(accum):
        key_heads = key_piece.reshape(count, num_heads, head_size)
        value_heads = value_piece.reshape(count, num_heads, head_size)
        scores = jnp.einsum(
            "qhd,khd->hqk", query_heads, key_heads, preferred_element_type=jnp.float32
        )
        key_place = lax.iota(jnp.int32, count)
        allowed = (key_place[None, :] <= query_place[:, None])[None]
        probs = jnp.where(allowed, jnp.exp(scores - log_total[:, :, None]), 0.0)
        d_prob = jnp.einsum(
            "qhd,khd->hqk", grad_heads, value_heads, preferred_element_type=jnp.float32
        )
        d_score = (probs * (d_prob - row_delta[:, :, None])).astype(jnp.bfloat16)
        added = jnp.einsum("hqk,khd->qhd", d_score, key_heads, preferred_element_type=jnp.float32)
        return added.reshape(group_rows, model_width)

    return lax.cond(
        jnp.int32(0) > first_row + group_rows - 1, lambda accum: accum, query_compute, empty
    )


def key_grads(k_low, v_low, q_low, d_mixed, total_all, delta_all, first_row, num_heads):
    group_rows, model_width = k_low.shape
    head_size = model_width // num_heads
    key_heads = k_low.reshape(group_rows, num_heads, head_size)
    value_heads = v_low.reshape(group_rows, num_heads, head_size)
    key_place = first_row + lax.iota(jnp.int32, group_rows)
    empty = jnp.zeros((group_rows, model_width), jnp.float32)
    query_piece = lax.all_gather(q_low, "seq", axis=0, tiled=True)
    grad_piece = lax.all_gather(d_mixed, "seq", axis=0, tiled=True)
    count = query_piece.shape[0]

    def key_compute(state):
        query_heads = query_piece.reshape(count, num_heads, head_size)
        grad_heads = grad_piece.reshape(count, num_heads, head_size)
        scores = jnp.einsum(
            "qhd,khd->hqk", query_heads, key_heads, preferred_element_type=jnp.float32
        )
        query_place = lax.iota(jnp.int32, count)
        allowed = (key_place[None, :] <= query_place[:, None])[None]
        probs = jnp.where(allowed, jnp.exp(scores - total_all[:, :, None]), 0.0)
        d_prob = jnp.einsum(
            "qhd,khd->hqk", grad_heads, value_heads, preferred_element_type=jnp.float32
        )
        d_score = (probs * (d_prob - delta_all[:, :, None])).astype(jnp.bfloat16)
        more_values = jnp.einsum(
            "hqk,qhd->khd",
            probs.astype(jnp.bfloat16),
            grad_heads,
            preferred_element_type=jnp.float32,
        )
        more_keys = jnp.einsum(
            "hqk,qhd->khd", d_score, query_heads, preferred_element_type=jnp.float32
        )
        return (
            more_keys.reshape(group_rows, model_width),
            more_values.reshape(group_rows, model_width),
        )

    return lax.cond(
        jnp.int32(0) + count - 1 < first_row, lambda state: state, key_compute, (empty, empty)
    )


def per_device(
    inputs,
    cotangent,
    w_query,
    w_key,
    w_value,
    w_out,
    w_up,
    w_down,
    norm_attn,
    norm_mlp,
    query_scale,
):
    micro_count, group_rows, model_width = inputs.shape
    num_heads = H
    head_size = model_width // num_heads
    first_row = lax.axis_index("seq") * group_rows
    results = []
    in_grads = []
    totals = None
    for micro_index in range(micro_count):
        gathered = (
            lax.all_gather(w_query, ("dp", "seq"), axis=0, tiled=True),
            lax.all_gather(w_key, ("dp", "seq"), axis=0, tiled=True),
            lax.all_gather(w_value, ("dp", "seq"), axis=0, tiled=True),
            lax.all_gather(w_out, ("dp", "seq"), axis=0, tiled=True),
            lax.all_gather(w_up, ("dp", "seq"), axis=0, tiled=True),
            lax.all_gather(w_down, ("dp", "seq"), axis=0, tiled=True),
            lax.all_gather(norm_attn, ("dp", "seq"), axis=0, tiled=True),
            lax.all_gather(norm_mlp, ("dp", "seq"), axis=0, tiled=True),
            lax.all_gather(query_scale, ("dp", "seq"), axis=0, tiled=True),
        )
        full_query, full_key, full_value, full_out, full_up, full_down = gathered[:6]
        gain_attn = gathered[6].astype(jnp.float32)
        gain_mlp = gathered[7].astype(jnp.float32)
        scale_param = gathered[8].astype(jnp.float32)
        scale = jax.nn.softplus(scale_param) * (SOFT_BASE / math.sqrt(head_size))
        layer_in = inputs[micro_index].astype(jnp.float32)
        inv_attn = lax.rsqrt(jnp.mean(layer_in * layer_in, axis=-1, keepdims=True) + EPS)
        normed_attn = layer_in * inv_attn
        h_attn = (normed_attn * gain_attn).astype(jnp.bfloat16)
        q_raw = jnp.dot(h_attn, full_query, preferred_element_type=jnp.float32)
        q_low = (q_raw * scale).astype(jnp.bfloat16)
        k_low = jnp.dot(h_attn, full_key, preferred_element_type=jnp.float32).astype(jnp.bfloat16)
        v_low = jnp.dot(h_attn, full_value, preferred_element_type=jnp.float32).astype(jnp.bfloat16)
        mixed, log_total = attend(q_low, k_low, v_low, first_row, num_heads)
        attn_in = mixed.astype(jnp.bfloat16)
        resid = layer_in + jnp.dot(attn_in, full_out, preferred_element_type=jnp.float32)
        inv_mlp = lax.rsqrt(jnp.mean(resid * resid, axis=-1, keepdims=True) + EPS)
        normed_mlp = resid * inv_mlp
        h_mlp = (normed_mlp * gain_mlp).astype(jnp.bfloat16)
        up_proj = jnp.dot(h_mlp, full_up, preferred_element_type=jnp.float32)
        activated = jax.nn.silu(up_proj).astype(jnp.bfloat16)
        layer_out = resid + jnp.dot(activated, full_down, preferred_element_type=jnp.float32)
        results.append(layer_out.astype(jnp.bfloat16))
        regathered = (
            lax.all_gather(w_query, ("dp", "seq"), axis=0, tiled=True),
            lax.all_gather(w_key, ("dp", "seq"), axis=0, tiled=True),
            lax.all_gather(w_value, ("dp", "seq"), axis=0, tiled=True),
            lax.all_gather(w_out, ("dp", "seq"), axis=0, tiled=True),
            lax.all_gather(w_up, ("dp", "seq"), axis=0, tiled=True),
            lax.all_gather(w_down, ("dp", "seq"), axis=0, tiled=True),
        )
        back_query, back_key, back_value, back_out, back_up, back_down = regathered
        cotan_rows = cotangent[micro_index]
        cotan_float = cotan_rows.astype(jnp.float32)
        grad_down = weight_outer(activated, cotan_rows)
        d_act = times_transpose(cotan_rows, back_down)
        sigmoid_up = jax.nn.sigmoid(up_proj)
        d_up = (d_act * sigmoid_up * (1.0 + up_proj * (1.0 - sigmoid_up))).astype(jnp.bfloat16)
        grad_up = weight_outer(h_mlp, d_up)
        d_hmlp = times_transpose(d_up, back_up)
        d_norm_mlp, grad_gain_mlp = norm_back(d_hmlp, normed_mlp, inv_mlp, gain_mlp)
        d_resid = cotan_float + d_norm_mlp
        resid_low = d_resid.astype(jnp.bfloat16)
        grad_out = weight_outer(attn_in, resid_low)
        d_mixed = times_transpose(resid_low, back_out).astype(jnp.bfloat16)
        row_delta = jnp.sum(
            (d_mixed.astype(jnp.float32) * mixed).reshape(group_rows, num_heads, head_size), axis=2
        ).T
        total_all, delta_all = (
            lax.all_gather(log_total, "seq", axis=1, tiled=True),
            lax.all_gather(row_delta, "seq", axis=1, tiled=True),
        )
        d_qlow = query_grads(
            q_low, d_mixed, k_low, v_low, log_total, row_delta, first_row, num_heads
        )
        d_keys, d_values = key_grads(
            k_low, v_low, q_low, d_mixed, total_all, delta_all, first_row, num_heads
        )
        keys_low = d_keys.astype(jnp.bfloat16)
        values_low = d_values.astype(jnp.bfloat16)
        d_qraw = (d_qlow * scale).astype(jnp.bfloat16)
        grad_scale = (
            jnp.sum(d_qlow * q_raw, axis=0)
            * jax.nn.sigmoid(scale_param)
            * (SOFT_BASE / math.sqrt(head_size))
        )
        grad_query = weight_outer(h_attn, d_qraw)
        grad_key = weight_outer(h_attn, keys_low)
        grad_value = weight_outer(h_attn, values_low)
        d_hattn = (
            times_transpose(d_qraw, back_query)
            + times_transpose(keys_low, back_key)
            + times_transpose(values_low, back_value)
        )
        d_norm_attn, grad_gain_attn = norm_back(d_hattn, normed_attn, inv_attn, gain_attn)
        in_grads.append(d_resid + d_norm_attn)
        grad_part = (
            grad_query,
            grad_key,
            grad_value,
            grad_out,
            grad_up,
            grad_down,
            grad_gain_attn,
            grad_gain_mlp,
            grad_scale,
        )
        if totals is None:
            totals = tuple(grad_part)
        else:
            totals = tuple((earlier + later for earlier, later in zip(totals, grad_part)))
    totals = (
        lax.psum_scatter(totals[0], ("dp", "seq"), scatter_dimension=0, tiled=True),
        lax.psum_scatter(totals[1], ("dp", "seq"), scatter_dimension=0, tiled=True),
        lax.psum_scatter(totals[2], ("dp", "seq"), scatter_dimension=0, tiled=True),
        lax.psum_scatter(totals[3], ("dp", "seq"), scatter_dimension=0, tiled=True),
        lax.psum_scatter(totals[4], ("dp", "seq"), scatter_dimension=0, tiled=True),
        lax.psum_scatter(totals[5], ("dp", "seq"), scatter_dimension=0, tiled=True),
        lax.psum_scatter(totals[6], ("dp", "seq"), scatter_dimension=0, tiled=True),
        lax.psum_scatter(totals[7], ("dp", "seq"), scatter_dimension=0, tiled=True),
        lax.psum_scatter(totals[8], ("dp", "seq"), scatter_dimension=0, tiled=True),
    )
    return (
        jnp.stack(results),
        jnp.stack(in_grads),
        totals[0],
        totals[1],
        totals[2],
        totals[3],
        totals[4],
        totals[5],
        totals[6],
        totals[7],
        totals[8],
    )


def solution(mesh):
    placed = (
        P("dp", "seq", None),
        P("dp", "seq", None),
        P(("dp", "seq"), None),
        P(("dp", "seq"), None),
        P(("dp", "seq"), None),
        P(("dp", "seq"), None),
        P(("dp", "seq"), None),
        P(("dp", "seq"), None),
        P(("dp", "seq")),
        P(("dp", "seq")),
        P(("dp", "seq")),
    )
    return jax.shard_map(
        per_device,
        mesh=mesh,
        in_specs=placed,
        out_specs=(
            P("dp", "seq", None),
            P("dp", "seq", None),
            P(("dp", "seq"), None),
            P(("dp", "seq"), None),
            P(("dp", "seq"), None),
            P(("dp", "seq"), None),
            P(("dp", "seq"), None),
            P(("dp", "seq"), None),
            P(("dp", "seq")),
            P(("dp", "seq")),
            P(("dp", "seq")),
        ),
        check_vma=False,
    )
```

profile of v0, /device:TPU:0, one launch (start us, length us, event | category | flops | bytes accessed | tf_op | source)
XLA Modules:
  0.0 1553.3 jit_solution(6274619430469553487)
XLA Ops:
  12.0 42.2 %all-reduce.7 = (bf16[1280]{0:T(1024)(128)(2,1)S(1)}, bf16[1280]{0:T(1024)(128)(2,1)S(1)}, bf16[1280]{0:T(1024)(128)(2,1)S(1)}) all-reduce(bf16[1280]{0:T(1024)(128)(2,1)S(1)} %dynamic-update-slice, bf16[1280]{0:T(1024)(128)(2,1)S(1)} %dynamic-update-slice.1, ...), channel_id=1, replica_groups=mesh['dp'=4,'seq'=8] {'dp','seq'}, use_global_device_ids=true, to_apply=%add | all-reduce | flops 3840 | bytes 15360
  55.5 17.4 %all-gather.15.cloned.1.call-done = bf16[1280,1280]{1,0:T(8,128)(2,1)} async-done(((bf16[40,1280]{1,0:T(8,128)(2,1)}), bf16[1280,1280]{1,0:T(8,128)(2,1)}) %all-gather.15.cloned.1.call-update) | async-done | bytes 3276816 | tf_op jit(solution)/shard_map/all_gather | solution.py:172
  76.5 57.7 %all-gather.21.cloned.1.call-done = bf16[1280,1280]{1,0:T(8,128)(2,1)} async-done(((bf16[40,1280]{1,0:T(8,128)(2,1)}), bf16[1280,1280]{1,0:T(8,128)(2,1)}) %all-gather.21.cloned.1.call-update) | async-done | bytes 3276816 | tf_op jit(solution)/shard_map/all_gather | solution.py:173
  146.4 48.9 %all-gather.19.cloned.1.call-done = bf16[1280,1280]{1,0:T(8,128)(2,1)} async-done(((bf16[40,1280]{1,0:T(8,128)(2,1)}), bf16[1280,1280]{1,0:T(8,128)(2,1)}) %all-gather.19.cloned.1.call-update) | async-done | bytes 3276816 | tf_op jit(solution)/shard_map/all_gather | solution.py:171
  203.1 26.5 %all-gather.31.cloned.1.call-done = bf16[1024,1280]{1,0:T(8,128)(2,1)} async-done(((bf16[128,1280]{1,0:T(8,128)(2,1)}), bf16[1024,1280]{1,0:T(8,128)(2,1)}) %all-gather.31.cloned.1.call-update) | async-done | bytes 2621456 | tf_op jit(solution)/shard_map/all_gather | solution.py:40
  229.6 34.4 %all-gather.33.cloned.1.call-done = bf16[1024,1280]{1,0:T(8,128)(2,1)} async-done(((bf16[128,1280]{1,0:T(8,128)(2,1)}), bf16[1024,1280]{1,0:T(8,128)(2,1)}) %all-gather.33.cloned.1.call-update) | async-done | bytes 2621456 | tf_op jit(solution)/shard_map/all_gather | solution.py:41
  264.0 18.8 %conditional.7 = (f32[16,128]{1,0:T(8,128)S(1)}, f32[16,128]{1,0:T(8,128)S(1)}, f32[16,128]{1,0:T(8,128)S(1)}, f32[128,1280]{1,0:T(8,128)S(1)}) conditional(s32[]{:T(128)} %convert_element_type.190, (s32[128]{0:T(128)S(1)}, bf16[1024,1280]{1,0:T(8,128)(2,1)}, bf16[128,16,80]{0,2,1:T(8,128)(2,1)}, bf16[1024,1280]{1,0:T(8,128)(2,1)}) %tuple.181, () %tuple.67), branch_computations={%region_7.10_spmd, %region_10.11_spmd} | conditional | flops 692357120 | bytes 87835224 | solution.py:67
  284.8 13.0 all-gather.17.cloned.1.call-done
  297.8 35.1 %all-gather.23.cloned.1.call-done = bf16[1024,1280]{1,0:T(8,128)(2,1)} async-done(((bf16[128,1280]{1,0:T(8,128)(2,1)}), bf16[1024,1280]{1,0:T(8,128)(2,1)}) %all-gather.23.cloned.1.call-update) | async-done | bytes 2621456 | tf_op jit(solution)/shard_map/all_gather | solution.py:41
  332.9 18.8 %conditional.6 = (f32[16,128]{1,0:T(8,128)S(1)}, f32[16,128]{1,0:T(8,128)S(1)}, f32[16,128]{1,0:T(8,128)S(1)}, f32[128,1280]{1,0:T(8,128)S(1)}) conditional(s32[]{:T(128)} %convert_element_type.190, (s32[128]{0:T(128)S(1)}, bf16[1024,1280]{1,0:T(8,128)(2,1)}, bf16[128,16,80]{0,2,1:T(8,128)(2,1)}, bf16[1024,1280]{1,0:T(8,128)(2,1)}) %tuple.179, () %tuple.65), branch_computations={%region_1.4_spmd, %region_4.5_spmd} | conditional | flops 692357120 | bytes 87835224 | solution.py:67
  355.7 38.4 %all-gather.25.cloned.1.call-done = bf16[1280,1280]{1,0:T(8,128)(2,1)} async-done(((bf16[40,1280]{1,0:T(8,128)(2,1)}), bf16[1280,1280]{1,0:T(8,128)(2,1)}) %all-gather.25.cloned.1.call-update) | async-done | bytes 3276816 | tf_op jit(solution)/shard_map/all_gather | solution.py:174
  397.8 57.5 %all-gather.27.cloned.1.call-done = bf16[1280,1280]{1,0:T(8,128)(2,1)} async-done(((bf16[40,1280]{1,0:T(8,128)(2,1)}), bf16[1280,1280]{1,0:T(8,128)(2,1)}) %all-gather.27.cloned.1.call-update) | async-done | bytes 3276816 | tf_op jit(solution)/shard_map/all_gather | solution.py:175
  458.7 57.6 %all-gather.29.cloned.1.call-done = bf16[1280,1280]{1,0:T(8,128)(2,1)} async-done(((bf16[40,1280]{1,0:T(8,128)(2,1)}), bf16[1280,1280]{1,0:T(8,128)(2,1)}) %all-gather.29.cloned.1.call-update) | async-done | bytes 3276816 | tf_op jit(solution)/shard_map/all_gather | solution.py:176
  542.6 26.9 %conditional.10 = (f32[128,1280]{1,0:T(8,128)S(1)}) conditional(s32[]{:T(128)} %convert_element_type.190, (s32[128]{0:T(128)S(1)}, bf16[1024,1280]{1,0:T(8,128)(2,1)}, bf16[128,16,80]{0,2,1:T(8,128)(2,1)S(1)}, f32[16,128]{1,0:T(8,128)S(1)}, bf16[128,1280]{1,0:T(8,128)(2,1)S(1)}, /*index=5*/bf16[1024,1280]{1,0:T(8,128)(2,1)}, ...), branch_computations={%region_21.22_spmd, %region_22.23_spmd} | conditional | flops 1017249792 | bytes 38683144 | solution.py:101
  558.5 9.6 fusion.53
  569.5 29.7 %conditional.8 = (f32[128,1280]{1,0:T(8,128)}) conditional(s32[]{:T(128)} %convert_element_type.190, (s32[128]{0:T(128)S(1)}, bf16[1024,1280]{1,0:T(8,128)(2,1)}, bf16[128,16,80]{0,2,1:T(8,128)(2,1)}, f32[16,128]{1,0:T(8,128)S(1)}, bf16[128,1280]{1,0:T(8,128)(2,1)}, /*index=5*/bf16[1024,1280]{1,0:T(8,128)(2,1)}, ...), branch_computations={%region_14.15_spmd, %region_15.16_spmd} | conditional | flops 1017249792 | bytes 38683144 | solution.py:101
  587.4 9.6 fusion.32
  624.6 15.4 all_gather.106
  640.0 15.1 all_gather.108
  655.0 13.9 all_gather.102
  669.0 14.8 all_gather.104
  683.8 35.7 %conditional.11 = (bf16[128,1280]{0,1:T(8,128)(2,1)}, bf16[128,1280]{0,1:T(8,128)(2,1)}) conditional(s32[]{:T(128)} %convert_element_type.218, (s32[128]{0:T(128)S(1)}, bf16[1024,1280]{1,0:T(8,128)(2,1)}, bf16[128,1280]{1,0:T(8,128)(2,1)}, f32[16,1024]{1,0:T(8,128)}, bf16[1024,1280]{1,0:T(8,128)(2,1)}, /*index=5*/bf16[128,1280]{1,0:T(8,128)(2,1)}, ...), branch_computations={%region_23.24_spmd, %region_24.25_spmd} | conditional | flops 1359413248 | bytes 49349136 | solution.py:144
  703.2 9.9 fusion.68
  719.5 32.6 %conditional.9 = (bf16[128,1280]{0,1:T(8,128)(2,1)S(1)}, bf16[128,1280]{0,1:T(8,128)(2,1)S(1)}) conditional(s32[]{:T(128)} %convert_element_type.218, (s32[128]{0:T(128)S(1)}, bf16[1024,1280]{1,0:T(8,128)(2,1)}, bf16[128,1280]{1,0:T(8,128)(2,1)S(1)}, f32[16,1024]{1,0:T(8,128)S(1)}, bf16[1024,1280]{1,0:T(8,128)(2,1)}, ...), branch_computations={%region_16.17_spmd, %region_17.18_spmd} | conditional | flops 1359413248 | bytes 49349136 | solution.py:144
  724.9 6.5 fusion.157
  737.0 9.2 fusion.47
  783.4 39.6 %all-reduce.6 = (f32[1280]{0:T(1024)S(1)}, f32[1280]{0:T(1024)S(1)}, f32[1280]{0:T(1024)S(1)}) all-reduce(f32[1280]{0:T(1024)S(1)} %add.209, f32[1280]{0:T(1024)S(1)} %add.210, f32[1280]{0:T(1024)S(1)} %fusion.131), channel_id=8, replica_groups=mesh['dp'=4,'seq'=8] {'dp','seq'}, use_global_device_ids=true, to_apply=%region_34.35.clone | all-reduce | flops 3840 | bytes 30720
  827.4 125.9 %reduce-scatter.13.cloned.1.call-done = f32[40,1280]{1,0:T(8,128)} async-done(((f32[1280,1280]{1,0:T(8,128)}), f32[40,1280]{1,0:T(8,128)}) %reduce-scatter.13.cloned.1.call-update) | async-done | bytes 204816 | tf_op jit(solution)/shard_map/reduce_scatter | solution.py:276
  953.3 147.9 %reduce-scatter.15.cloned.1.call-done = f32[40,1280]{1,0:T(8,128)} async-done(((f32[1280,1280]{1,0:T(8,128)}), f32[40,1280]{1,0:T(8,128)}) %reduce-scatter.15.cloned.1.call-update) | async-done | bytes 204816 | tf_op jit(solution)/shard_map/reduce_scatter | solution.py:277
  1101.2 147.9 %reduce-scatter.17.cloned.1.call-done = f32[40,1280]{1,0:T(8,128)} async-done(((f32[1280,1280]{1,0:T(8,128)}), f32[40,1280]{1,0:T(8,128)}) %reduce-scatter.17.cloned.1.call-update) | async-done | bytes 204816 | tf_op jit(solution)/shard_map/reduce_scatter | solution.py:278
  1249.1 148.5 %reduce-scatter.9.cloned.1.call-done = f32[40,1280]{1,0:T(8,128)} async-done(((f32[1280,1280]{1,0:T(8,128)}), f32[40,1280]{1,0:T(8,128)}) %reduce-scatter.9.cloned.1.call-update) | async-done | bytes 204816 | tf_op jit(solution)/shard_map/reduce_scatter | solution.py:274
  1397.6 148.6 %reduce-scatter.11.cloned.1.call-done = f32[40,1280]{1,0:T(8,128)} async-done(((f32[1280,1280]{1,0:T(8,128)}), f32[40,1280]{1,0:T(8,128)}) %reduce-scatter.11.cloned.1.call-update) | async-done | bytes 204816 | tf_op jit(solution)/shard_map/reduce_scatter | solution.py:275
  (256 shorter events, 246.6 us)
Async XLA Ops:
  7.2 127.0 %copy-start = (bf16[2,128,1280]{2,1,0:T(8,128)(2,1)S(1)}, bf16[2,128,1280]{2,1,0:T(8,128)(2,1)}, u32[]{:S(2)}) copy-start(bf16[2,128,1280]{2,1,0:T(8,128)(2,1)} %param.23) | copy-start | bytes 1966084
  7.2 65.8 %all-gather.15.cloned.1.call-start = ((), (), s32[]{:S(2)}) async-start(), calls=%async_computation.6 | async-start | bytes 3379200 | tf_op jit(solution)/shard_map/all_gather | solution.py:172
  7.9 126.2 %all-gather.21.cloned.1.call-start = ((), (), s32[]{:S(2)}) async-start(), calls=%async_computation.9 | async-start | bytes 3379200 | tf_op jit(solution)/shard_map/all_gather | solution.py:173
  8.7 186.6 %all-gather.19.cloned.1.call-start = ((), (), s32[]{:S(2)}) async-start(), calls=%async_computation.8 | async-start | bytes 3379200 | tf_op jit(solution)/shard_map/all_gather | solution.py:171
  9.4 220.2 %all-gather.31.cloned.1.call-start = ((), (), s32[]{:S(2)}) async-start(), calls=%async_computation.14 | async-start | bytes 2949120 | tf_op jit(solution)/shard_map/all_gather | solution.py:40
  54.2 92.1 %copy-start.40 = (bf16[1280]{0:T(1024)(128)(2,1)}, bf16[1280]{0:T(1024)(128)(2,1)S(1)}, u32[]{:S(2)}) copy-start(bf16[1280]{0:T(1024)(128)(2,1)S(1)} %get-tuple-element.289) | copy-start | bytes 7684
  76.4 187.6 %all-gather.33.cloned.1.call-start = ((), (), s32[]{:S(2)}) async-start(), calls=%async_computation.15 | async-start | bytes 2949120 | tf_op jit(solution)/shard_map/all_gather | solution.py:41
  137.5 160.3 %all-gather.17.cloned.1.call-start = ((), (), s32[]{:S(2)}) async-start(), calls=%async_computation.7 | async-start | bytes 2949120 | tf_op jit(solution)/shard_map/all_gather | solution.py:40
  140.9 192.1 %all-gather.23.cloned.1.call-start = ((), (), s32[]{:S(2)}) async-start(), calls=%async_computation.10 | async-start | bytes 2949120 | tf_op jit(solution)/shard_map/all_gather | solution.py:41
  144.2 250.0 %all-gather.25.cloned.1.call-start = ((), (), s32[]{:S(2)}) async-start(), calls=%async_computation.11 | async-start | bytes 3379200 | tf_op jit(solution)/shard_map/all_gather | solution.py:174
  145.0 310.4 %all-gather.27.cloned.1.call-start = ((), (), s32[]{:S(2)}) async-start(), calls=%async_computation.12 | async-start | bytes 3379200 | tf_op jit(solution)/shard_map/all_gather | solution.py:175
  145.7 370.6 %all-gather.29.cloned.1.call-start = ((), (), s32[]{:S(2)}) async-start(), calls=%async_computation.13 | async-start | bytes 3379200 | tf_op jit(solution)/shard_map/all_gather | solution.py:176
  146.3 537.5 %all-gather.39.cloned.1.call-start = ((), (), s32[]{:S(2)}) async-start(), calls=%async_computation.18 | async-start | bytes 2949120 | tf_op jit(solution)/shard_map/all_gather | solution.py:113
  199.8 64.2 %copy-start.26 = (bf16[128,1280]{1,0:T(8,128)(2,1)}, bf16[128,1280]{1,0:T(8,128)(2,1)S(1)}, u32[]{:S(2)}) copy-start(bf16[128,1280]{1,0:T(8,128)(2,1)S(1)} %get-tuple-element.305) | copy-start | bytes 983044
  199.8 484.0 %all-gather.41.cloned.1.call-start = ((), (), s32[]{:S(2)}) async-start(), calls=%async_computation.19 | async-start | bytes 2949120 | tf_op jit(solution)/shard_map/all_gather | solution.py:114
  269.6 3.8 copy-start.8
  354.3 173.0 %copy-start.10 = (f32[128,1280]{1,0:T(8,128)}, f32[128,1280]{1,0:T(8,128)S(1)}, u32[]{:S(2)}) copy-start(f32[128,1280]{1,0:T(8,128)S(1)} %div.48) | copy-start | bytes 1966084
  530.6 188.9 %all-gather.35.cloned.1.call-start = ((), (), s32[]{:S(2)}) async-start(), calls=%async_computation.16 | async-start | bytes 2949120 | tf_op jit(solution)/shard_map/all_gather | solution.py:113
  531.3 188.2 %all-gather.37.cloned.1.call-start = ((), (), s32[]{:S(2)}) async-start(), calls=%async_computation.17 | async-start | bytes 2949120 | tf_op jit(solution)/shard_map/all_gather | solution.py:114
  535.8 6.8 copy-start.23
  535.8 6.8 copy-start.27
  535.8 291.6 %reduce-scatter.7.cloned.1.call-start = ((), (), s32[]{:S(2)}) async-start(), calls=%async_computation.20 | async-start | bytes 6758400 | tf_op jit(solution)/shard_map/reduce_scatter | solution.py:273
  605.2 348.0 %reduce-scatter.13.cloned.1.call-start = ((), (), s32[]{:S(2)}) async-start(), calls=%async_computation.23 | async-start | bytes 6758400 | tf_op jit(solution)/shard_map/reduce_scatter | solution.py:276
  611.4 489.8 %reduce-scatter.15.cloned.1.call-start = ((), (), s32[]{:S(2)}) async-start(), calls=%async_computation.24 | async-start | bytes 6758400 | tf_op jit(solution)/shard_map/reduce_scatter | solution.py:277
  617.4 631.8 %reduce-scatter.17.cloned.1.call-start = ((), (), s32[]{:S(2)}) async-start(), calls=%async_computation.25 | async-start | bytes 6758400 | tf_op jit(solution)/shard_map/reduce_scatter | solution.py:278
  624.5 773.1 %reduce-scatter.9.cloned.1.call-start = ((), (), s32[]{:S(2)}) async-start(), calls=%async_computation.21 | async-start | bytes 6758400 | tf_op jit(solution)/shard_map/reduce_scatter | solution.py:274
  683.8 35.7 %copy-start.24 = (bf16[128,1280]{1,0:T(8,128)(2,1)S(1)}, bf16[128,1280]{1,0:T(8,128)(2,1)}, u32[]{:S(2)}) copy-start(bf16[128,1280]{1,0:T(8,128)(2,1)} %convolution_convert_fusion.5) | copy-start | bytes 983044
  683.8 35.7 %copy-start.25 = (bf16[128,1280]{1,0:T(8,128)(2,1)S(1)}, bf16[128,1280]{1,0:T(8,128)(2,1)}, u32[]{:S(2)}) copy-start(bf16[128,1280]{1,0:T(8,128)(2,1)} %convolution_convert_fusion.4) | copy-start | bytes 983044
  752.2 6.1 copy-start.34
  758.2 788.1 %reduce-scatter.11.cloned.1.call-start = ((), (), s32[]{:S(2)}) async-start(), calls=%async_computation.22 | async-start | bytes 6758400 | tf_op jit(solution)/shard_map/reduce_scatter | solution.py:275
  781.1 43.6 %copy-start.15 = (f32[128,1280]{1,0:T(8,128)S(1)}, f32[128,1280]{1,0:T(8,128)}, u32[]{:S(2)}) copy-start(f32[128,1280]{1,0:T(8,128)} %copy-done.13) | copy-start | bytes 1966084
  781.1 43.6 %copy-start.18 = (f32[128,1280]{1,0:T(8,128)S(1)}, f32[128,1280]{1,0:T(8,128)}, u32[]{:S(2)}) copy-start(f32[128,1280]{1,0:T(8,128)} %get-tuple-element.301) | copy-start | bytes 1966084
  (32 other events, 71.4 us)
Sparse Core Ops, SparseCore 0:
  10.9 62.0 all-gather.14
  75.8 58.2 all-gather.20
  137.0 58.2 all-gather.18
  196.8 32.7 all-gather.30
  231.1 32.8 all-gather.32
  265.5 32.2 all-gather.16
  299.4 33.4 all-gather.22
  335.8 58.3 all-gather.24
  397.0 58.2 all-gather.26
  458.0 58.2 all-gather.28
  518.0 32.7 all-gather.38
  552.3 32.8 all-gather.40
  586.8 32.8 all-gather.34
  621.2 33.7 all-gather.36
  657.7 147.1 reduce-scatter.6
  807.7 145.5 reduce-scatter.12
  956.0 145.1 reduce-scatter.14
  1103.9 145.1 reduce-scatter.16
  1252.0 145.5 reduce-scatter.8
  1400.3 145.8 reduce-scatter.10
where the time goes:
time: 1560 us; the launch traced here: 1550 us
  waiting for transfers between devices  1110 us (71%)
  matrix products  182 us (12%)
  blocking collectives  141 us (9%)
  local copies, waits for them, and re-layouts  84 us (5%)
  other arithmetic  19.1 us (1%)
    reduce_scatter x1, waiting for transfers between devices, per_device(): lax.psum_scatter(totals[2], ('dp', 'seq'), scatter_dimension=0, tiled=True)  149 us
    reduce_scatter x1, waiting for transfers between devices, per_device(): lax.psum_scatter(totals[1], ('dp', 'seq'), scatter_dimension=0, tiled=True)  148 us
    reduce_scatter x1, waiting for transfers between devices, per_device(): lax.psum_scatter(totals[5], ('dp', 'seq'), scatter_dimension=0, tiled=True)  148 us
    reduce_scatter x1, waiting for transfers between devices, per_device(): lax.psum_scatter(totals[4], ('dp', 'seq'), scatter_dimension=0, tiled=True)  148 us
    reduce_scatter x1, waiting for transfers between devices, per_device(): lax.psum_scatter(totals[3], ('dp', 'seq'), scatter_dimension=0, tiled=True)  126 us
    unnamed x2, blocking collectives  81.8 us
    all_gather x2, waiting for transfers between devices, attend(): value_piece = lax.all_gather(v_low, 'seq', axis=0, tiled=True)  69.5 us
    all_gather x1, waiting for transfers between devices, per_device(): lax.all_gather(w_value, ('dp', 'seq'), axis=0, tiled=True)  57.7 us
  transfers between devices with their start and end apart: 20, of which 15 were waited for; matrix products, arithmetic and copies ran while one was open for 18% of the time, Pallas kernels for 0%

commit v1 on v0

--- a/solution.py
+++ b/solution.py
@@ -37,8 +37,11 @@
         jnp.zeros((num_heads, group_rows), jnp.float32),
         jnp.zeros((group_rows, model_width), jnp.float32),
     )
-    key_piece = lax.all_gather(k_low, "seq", axis=0, tiled=True)
-    value_piece = lax.all_gather(v_low, "seq", axis=0, tiled=True)
+    key_piece, value_piece = jnp.split(
+        lax.all_gather(jnp.concatenate([k_low, v_low], axis=1), "seq", axis=0, tiled=True),
+        [k_low.shape[1]],
+        axis=1,
+    )
     count = key_piece.shape[0]
 
     def attend_compute(state):

time: 1560 us -> 1670 us (1.071)
  waiting for transfers between devices: 1110 us -> 1230 us
    all_gather x4 -> x6, waiting for transfers between devices: 109 us -> 171 us  [the longest x2 85.9 us: attend(): lax.all_gather(jnp.concatenate([k_low, v_low], axis=1), 'seq', axis=0, ti...]
    all_gather x1, waiting for transfers between devices: 17.4 us -> 58.4 us  [per_device(): lax.all_gather(w_key, ('dp', 'seq'), axis=0, tiled=True)]
    all_gather x1, waiting for transfers between devices: 57.7 us -> 17.5 us  [per_device(): lax.all_gather(w_value, ('dp', 'seq'), axis=0, tiled=True)]
    reduce_scatter x1, waiting for transfers between devices: 0.01 us -> 31.5 us  [per_device(): lax.psum_scatter(totals[0], ('dp', 'seq'), scatter_dimension=0, tiled=True)]
    reduce_scatter x1, waiting for transfers between devices: 126 us -> 148 us  [per_device(): lax.psum_scatter(totals[3], ('dp', 'seq'), scatter_dimension=0, tiled=True)]
    another operation x18 -> x16, local copies, waits for them, and re-layouts: 55.9 us -> 59.5 us
  transfers between devices with their start and end apart: 20 -> 22, of which waited for: 15 -> 18; matrix products, arithmetic and copies ran while one was open for 18% -> 16% of each run, Pallas kernels for 0% -> 0%
where the time goes in v1:
time: 1670 us
  waiting for transfers between devices  1230 us (74%)
  matrix products  171 us (10%)
  blocking collectives  141 us (8%)
  local copies, waits for them, and re-layouts  90.9 us (5%)
  other arithmetic  21 us (1%)
    reduce_scatter x1, waiting for transfers between devices, per_device(): lax.psum_scatter(totals[2], ('dp', 'seq'), scatter_dimension=0, tiled=True)  149 us
    reduce_scatter x1, waiting for transfers between devices, per_device(): lax.psum_scatter(totals[5], ('dp', 'seq'), scatter_dimension=0, tiled=True)  149 us
    reduce_scatter x1, waiting for transfers between devices, per_device(): lax.psum_scatter(totals[3], ('dp', 'seq'), scatter_dimension=0, tiled=True)  148 us
    reduce_scatter x1, waiting for transfers between devices, per_device(): lax.psum_scatter(totals[4], ('dp', 'seq'), scatter_dimension=0, tiled=True)  148 us
    reduce_scatter x1, waiting for transfers between devices, per_device(): lax.psum_scatter(totals[1], ('dp', 'seq'), scatter_dimension=0, tiled=True)  148 us
    all_gather x2, waiting for transfers between devices, attend(): lax.all_gather(jnp.concatenate([k_low, v_low], axis=1), 'seq', axis=0, ti...  85.9 us
    unnamed x2, blocking collectives  81.9 us
    all_gather x2, waiting for transfers between devices, query_grads(): value_piece = lax.all_gather(v_low, 'seq', axis=0, tiled=True)  68.8 us
  transfers between devices with their start and end apart: 22, of which 18 were waited for; matrix products, arithmetic and copies ran while one was open for 16% of the time, Pallas kernels for 0%

profile of v1, /device:TPU:0, one launch (start us, length us, event | category | flops | bytes accessed | tf_op | source)
XLA Modules:
  0.0 1666.5 jit_solution(5846346032747064047)
XLA Ops:
  12.0 42.2 %all-reduce.7 = (bf16[1280]{0:T(1024)(128)(2,1)S(1)}, bf16[1280]{0:T(1024)(128)(2,1)S(1)}, bf16[1280]{0:T(1024)(128)(2,1)S(1)}) all-reduce(bf16[1280]{0:T(1024)(128)(2,1)S(1)} %dynamic-update-slice, bf16[1280]{0:T(1024)(128)(2,1)S(1)} %dynamic-update-slice.1, ...), channel_id=1, replica_groups=mesh['dp'=4,'seq'=8] {'dp','seq'}, use_global_device_ids=true, to_apply=%add | all-reduce | flops 3840 | bytes 15360
  55.5 17.5 %all-gather.19.cloned.1.call-done = bf16[1280,1280]{1,0:T(8,128)(2,1)} async-done(((bf16[40,1280]{1,0:T(8,128)(2,1)}), bf16[1280,1280]{1,0:T(8,128)(2,1)}) %all-gather.19.cloned.1.call-update) | async-done | bytes 3276816 | tf_op jit(solution)/shard_map/all_gather | solution.py:176
  75.7 58.4 %all-gather.17.cloned.1.call-done = bf16[1280,1280]{1,0:T(8,128)(2,1)} async-done(((bf16[40,1280]{1,0:T(8,128)(2,1)}), bf16[1280,1280]{1,0:T(8,128)(2,1)}) %all-gather.17.cloned.1.call-update) | async-done | bytes 3276816 | tf_op jit(solution)/shard_map/all_gather | solution.py:175
  148.8 46.5 %all-gather.23.cloned.1.call-done = bf16[1280,1280]{1,0:T(8,128)(2,1)} async-done(((bf16[40,1280]{1,0:T(8,128)(2,1)}), bf16[1280,1280]{1,0:T(8,128)(2,1)}) %all-gather.23.cloned.1.call-update) | async-done | bytes 3276816 | tf_op jit(solution)/shard_map/all_gather | solution.py:174
  202.5 49.8 %all-gather.31.cloned.1.call-done = bf16[1024,2560]{1,0:T(8,128)(2,1)} async-done(((bf16[128,2560]{1,0:T(8,128)(2,1)}), bf16[1024,2560]{1,0:T(8,128)(2,1)}) %all-gather.31.cloned.1.call-update) | async-done | bytes 5242896 | tf_op jit(solution)/shard_map/all_gather | solution.py:41
  252.3 19.1 %conditional.7 = (f32[16,128]{1,0:T(8,128)S(1)}, f32[16,128]{1,0:T(8,128)S(1)}, f32[16,128]{1,0:T(8,128)S(1)}, f32[128,1280]{1,0:T(8,128)S(1)}) conditional(s32[]{:T(128)} %convert_element_type.190, (s32[128]{0:T(128)S(1)}, bf16[1024,2560]{1,0:T(8,128)(2,1)}, bf16[128,16,80]{0,2,1:T(8,128)(2,1)}) %tuple.66, () %tuple.67), branch_computations={%region_7.10_spmd, %region_10.11_spmd} | conditional | flops 692357120 | bytes 54280736 | solution.py:70
  272.6 36.1 %all-gather.21.cloned.1.call-done = bf16[1024,2560]{1,0:T(8,128)(2,1)} async-done(((bf16[128,2560]{1,0:T(8,128)(2,1)}), bf16[1024,2560]{1,0:T(8,128)(2,1)}) %all-gather.21.cloned.1.call-update) | async-done | bytes 5242896 | tf_op jit(solution)/shard_map/all_gather | solution.py:41
  308.7 18.0 %conditional.6 = (f32[16,128]{1,0:T(8,128)S(1)}, f32[16,128]{1,0:T(8,128)S(1)}, f32[16,128]{1,0:T(8,128)S(1)}, f32[128,1280]{1,0:T(8,128)S(1)}) conditional(s32[]{:T(128)} %convert_element_type.190, (s32[128]{0:T(128)S(1)}, bf16[1024,2560]{1,0:T(8,128)(2,1)}, bf16[128,16,80]{0,2,1:T(8,128)(2,1)S(1)}) %tuple.189, () %tuple.65), branch_computations={%region_1.4_spmd, %region_4.5_spmd} | conditional | flops 692357120 | bytes 54280736 | solution.py:70
  331.4 38.1 %all-gather.25.cloned.1.call-done = bf16[1280,1280]{1,0:T(8,128)(2,1)} async-done(((bf16[40,1280]{1,0:T(8,128)(2,1)}), bf16[1280,1280]{1,0:T(8,128)(2,1)}) %all-gather.25.cloned.1.call-update) | async-done | bytes 3276816 | tf_op jit(solution)/shard_map/all_gather | solution.py:177
  373.2 57.5 %all-gather.27.cloned.1.call-done = bf16[1280,1280]{1,0:T(8,128)(2,1)} async-done(((bf16[40,1280]{1,0:T(8,128)(2,1)}), bf16[1280,1280]{1,0:T(8,128)(2,1)}) %all-gather.27.cloned.1.call-update) | async-done | bytes 3276816 | tf_op jit(solution)/shard_map/all_gather | solution.py:178
  434.1 57.7 %all-gather.29.cloned.1.call-done = bf16[1280,1280]{1,0:T(8,128)(2,1)} async-done(((bf16[40,1280]{1,0:T(8,128)(2,1)}), bf16[1280,1280]{1,0:T(8,128)(2,1)}) %all-gather.29.cloned.1.call-update) | async-done | bytes 3276816 | tf_op jit(solution)/shard_map/all_gather | solution.py:179
  526.3 34.4 %all-gather.43.cloned.1.call-done = bf16[1024,1280]{1,0:T(8,128)(2,1)} async-done(((bf16[128,1280]{1,0:T(8,128)(2,1)}), bf16[1024,1280]{1,0:T(8,128)(2,1)}) %all-gather.43.cloned.1.call-update) | async-done | bytes 2621456 | tf_op jit(solution)/shard_map/all_gather | solution.py:85
  560.7 26.9 %conditional.10 = (f32[128,1280]{1,0:T(8,128)S(1)}) conditional(s32[]{:T(128)} %convert_element_type.190, (s32[128]{0:T(128)S(1)}, bf16[1024,1280]{1,0:T(8,128)(2,1)}, bf16[128,16,80]{0,2,1:T(8,128)(2,1)}, f32[16,128]{1,0:T(8,128)S(1)}, bf16[128,1280]{1,0:T(8,128)(2,1)S(1)}, /*index=5*/bf16[1024,1280]{1,0:T(8,128)(2,1)}, ...), branch_computations={%region_21.22_spmd, %region_22.23_spmd} | conditional | flops 1017249792 | bytes 38683144 | solution.py:104
  576.7 9.6 fusion.53
  595.2 34.4 %all-gather.35.cloned.1.call-done = bf16[1024,1280]{1,0:T(8,128)(2,1)} async-done(((bf16[128,1280]{1,0:T(8,128)(2,1)}), bf16[1024,1280]{1,0:T(8,128)(2,1)}) %all-gather.35.cloned.1.call-update) | async-done | bytes 2621456 | tf_op jit(solution)/shard_map/all_gather | solution.py:85
  629.6 29.8 %conditional.8 = (f32[128,1280]{1,0:T(8,128)}) conditional(s32[]{:T(128)} %convert_element_type.190, (s32[128]{0:T(128)S(1)}, bf16[1024,1280]{1,0:T(8,128)(2,1)}, bf16[128,16,80]{0,2,1:T(8,128)(2,1)}, f32[16,128]{1,0:T(8,128)S(1)}, bf16[128,1280]{1,0:T(8,128)(2,1)}, /*index=5*/bf16[1024,1280]{1,0:T(8,128)(2,1)}, ...), branch_computations={%region_14.15_spmd, %region_15.16_spmd} | conditional | flops 1017249792 | bytes 38683144 | solution.py:104
  647.5 9.8 fusion.32
  684.8 15.2 all_gather.110
  700.0 14.9 all_gather.112
  714.9 14.1 all_gather.104
  729.0 14.9 all_gather.106
  743.8 35.8 %conditional.11 = (bf16[128,1280]{0,1:T(8,128)(2,1)}, bf16[128,1280]{0,1:T(8,128)(2,1)}) conditional(s32[]{:T(128)} %convert_element_type.218, (s32[128]{0:T(128)S(1)}, bf16[1024,1280]{1,0:T(8,128)(2,1)}, bf16[128,1280]{1,0:T(8,128)(2,1)}, f32[16,1024]{1,0:T(8,128)}, bf16[1024,1280]{1,0:T(8,128)(2,1)}, /*index=5*/bf16[128,1280]{1,0:T(8,128)(2,1)}, ...), branch_computations={%region_23.24_spmd, %region_24.25_spmd} | conditional | flops 1359413248 | bytes 49349136 | solution.py:147
  763.3 9.8 fusion.68
  779.6 31.9 %conditional.9 = (bf16[128,1280]{0,1:T(8,128)(2,1)S(1)}, bf16[128,1280]{0,1:T(8,128)(2,1)S(1)}) conditional(s32[]{:T(128)} %convert_element_type.218, (s32[128]{0:T(128)S(1)}, bf16[1024,1280]{1,0:T(8,128)(2,1)}, bf16[128,1280]{1,0:T(8,128)(2,1)S(1)}, f32[16,1024]{1,0:T(8,128)S(1)}, bf16[1024,1280]{1,0:T(8,128)(2,1)}, ...), branch_computations={%region_16.17_spmd, %region_17.18_spmd} | conditional | flops 1359413248 | bytes 49349136 | solution.py:147
  796.3 9.2 fusion.47
  842.7 39.7 %all-reduce.6 = (f32[1280]{0:T(1024)S(1)}, f32[1280]{0:T(1024)S(1)}, f32[1280]{0:T(1024)S(1)}) all-reduce(f32[1280]{0:T(1024)S(1)} %add.209, f32[1280]{0:T(1024)S(1)} %add.210, f32[1280]{0:T(1024)S(1)} %fusion.131), channel_id=8, replica_groups=mesh['dp'=4,'seq'=8] {'dp','seq'}, use_global_device_ids=true, to_apply=%region_34.35.clone | all-reduce | flops 3840 | bytes 30720
  886.8 31.5 %reduce-scatter.7.cloned.1.call-done = f32[40,1280]{1,0:T(8,128)} async-done(((f32[1280,1280]{1,0:T(8,128)}), f32[40,1280]{1,0:T(8,128)}) %reduce-scatter.7.cloned.1.call-update) | async-done | bytes 204816 | tf_op jit(solution)/shard_map/reduce_scatter | solution.py:276
  918.4 148.5 %reduce-scatter.13.cloned.1.call-done = f32[40,1280]{1,0:T(8,128)} async-done(((f32[1280,1280]{1,0:T(8,128)}), f32[40,1280]{1,0:T(8,128)}) %reduce-scatter.13.cloned.1.call-update) | async-done | bytes 204816 | tf_op jit(solution)/shard_map/reduce_scatter | solution.py:279
  1066.8 147.8 %reduce-scatter.15.cloned.1.call-done = f32[40,1280]{1,0:T(8,128)} async-done(((f32[1280,1280]{1,0:T(8,128)}), f32[40,1280]{1,0:T(8,128)}) %reduce-scatter.15.cloned.1.call-update) | async-done | bytes 204816 | tf_op jit(solution)/shard_map/reduce_scatter | solution.py:280
  1214.7 148.5 %reduce-scatter.17.cloned.1.call-done = f32[40,1280]{1,0:T(8,128)} async-done(((f32[1280,1280]{1,0:T(8,128)}), f32[40,1280]{1,0:T(8,128)}) %reduce-scatter.17.cloned.1.call-update) | async-done | bytes 204816 | tf_op jit(solution)/shard_map/reduce_scatter | solution.py:281
  1363.2 147.7 %reduce-scatter.9.cloned.1.call-done = f32[40,1280]{1,0:T(8,128)} async-done(((f32[1280,1280]{1,0:T(8,128)}), f32[40,1280]{1,0:T(8,128)}) %reduce-scatter.9.cloned.1.call-update) | async-done | bytes 204816 | tf_op jit(solution)/shard_map/reduce_scatter | solution.py:277
  1510.8 148.6 %reduce-scatter.11.cloned.1.call-done = f32[40,1280]{1,0:T(8,128)} async-done(((f32[1280,1280]{1,0:T(8,128)}), f32[40,1280]{1,0:T(8,128)}) %reduce-scatter.11.cloned.1.call-update) | async-done | bytes 204816 | tf_op jit(solution)/shard_map/reduce_scatter | solution.py:278
  (266 shorter events, 268.5 us)
Async XLA Ops:
  7.2 127.0 %copy-start = (bf16[2,128,1280]{2,1,0:T(8,128)(2,1)S(1)}, bf16[2,128,1280]{2,1,0:T(8,128)(2,1)}, u32[]{:S(2)}) copy-start(bf16[2,128,1280]{2,1,0:T(8,128)(2,1)} %param.23) | copy-start | bytes 1966084
  7.2 65.8 %all-gather.19.cloned.1.call-start = ((), (), s32[]{:S(2)}) async-start(), calls=%async_computation.7 | async-start | bytes 3379200 | tf_op jit(solution)/shard_map/all_gather | solution.py:176
  7.9 126.2 %all-gather.17.cloned.1.call-start = ((), (), s32[]{:S(2)}) async-start(), calls=%async_computation.6 | async-start | bytes 3379200 | tf_op jit(solution)/shard_map/all_gather | solution.py:175
  8.7 186.6 %all-gather.23.cloned.1.call-start = ((), (), s32[]{:S(2)}) async-start(), calls=%async_computation.9 | async-start | bytes 3379200 | tf_op jit(solution)/shard_map/all_gather | solution.py:174
  9.4 242.9 %all-gather.31.cloned.1.call-start = ((), (), s32[]{:S(2)}) async-start(), calls=%async_computation.13 | async-start | bytes 5898240 | tf_op jit(solution)/shard_map/all_gather | solution.py:41
  54.2 94.6 %copy-start.41 = (bf16[1280]{0:T(1024)(128)(2,1)}, bf16[1280]{0:T(1024)(128)(2,1)S(1)}, u32[]{:S(2)}) copy-start(bf16[1280]{0:T(1024)(128)(2,1)S(1)} %get-tuple-element.283) | copy-start | bytes 7684
  75.7 64.6 %copy-start.20 = (bf16[128,1280]{1,0:T(8,128)(2,1)}, bf16[128,1280]{1,0:T(8,128)(2,1)S(1)}, u32[]{:S(2)}) copy-start(bf16[128,1280]{1,0:T(8,128)(2,1)S(1)} %convolution_convert_fusion.2) | copy-start | bytes 983044
  137.7 171.0 %all-gather.21.cloned.1.call-start = ((), (), s32[]{:S(2)}) async-start(), calls=%async_computation.8 | async-start | bytes 5898240 | tf_op jit(solution)/shard_map/all_gather | solution.py:41
  144.0 225.5 %all-gather.25.cloned.1.call-start = ((), (), s32[]{:S(2)}) async-start(), calls=%async_computation.10 | async-start | bytes 3379200 | tf_op jit(solution)/shard_map/all_gather | solution.py:177
  144.6 286.1 %all-gather.27.cloned.1.call-start = ((), (), s32[]{:S(2)}) async-start(), calls=%async_computation.11 | async-start | bytes 3379200 | tf_op jit(solution)/shard_map/all_gather | solution.py:178
  145.3 346.5 %all-gather.29.cloned.1.call-start = ((), (), s32[]{:S(2)}) async-start(), calls=%async_computation.12 | async-start | bytes 3379200 | tf_op jit(solution)/shard_map/all_gather | solution.py:179
  146.1 380.2 %all-gather.41.cloned.1.call-start = ((), (), s32[]{:S(2)}) async-start(), calls=%async_computation.18 | async-start | bytes 2949120 | tf_op jit(solution)/shard_map/all_gather | solution.py:84
  146.8 413.9 %all-gather.43.cloned.1.call-start = ((), (), s32[]{:S(2)}) async-start(), calls=%async_computation.19 | async-start | bytes 2949120 | tf_op jit(solution)/shard_map/all_gather | solution.py:85
  147.4 447.8 %all-gather.33.cloned.1.call-start = ((), (), s32[]{:S(2)}) async-start(), calls=%async_computation.14 | async-start | bytes 2949120 | tf_op jit(solution)/shard_map/all_gather | solution.py:84
  148.2 481.5 %all-gather.35.cloned.1.call-start = ((), (), s32[]{:S(2)}) async-start(), calls=%async_computation.15 | async-start | bytes 2949120 | tf_op jit(solution)/shard_map/all_gather | solution.py:85
  148.7 595.1 %all-gather.45.cloned.1.call-start = ((), (), s32[]{:S(2)}) async-start(), calls=%async_computation.20 | async-start | bytes 2949120 | tf_op jit(solution)/shard_map/all_gather | solution.py:116
  199.8 52.5 %copy-start.26 = (bf16[128,1280]{1,0:T(8,128)(2,1)}, bf16[128,1280]{1,0:T(8,128)(2,1)S(1)}, u32[]{:S(2)}) copy-start(bf16[128,1280]{1,0:T(8,128)(2,1)S(1)} %get-tuple-element.303) | copy-start | bytes 983044
  199.8 544.0 %all-gather.47.cloned.1.call-start = ((), (), s32[]{:S(2)}) async-start(), calls=%async_computation.21 | async-start | bytes 2949120 | tf_op jit(solution)/shard_map/all_gather | solution.py:117
  202.5 106.2 %copy-start.25 = (bf16[128,1280]{0,1:T(8,128)(2,1)}, bf16[128,1280]{0,1:T(8,128)(2,1)S(1)}, u32[]{:S(2)}) copy-start(bf16[128,1280]{0,1:T(8,128)(2,1)S(1)} %copy.72) | copy-start | bytes 983044
  329.8 173.1 %copy-start.8 = (f32[128,1280]{1,0:T(8,128)}, f32[128,1280]{1,0:T(8,128)S(1)}, u32[]{:S(2)}) copy-start(f32[128,1280]{1,0:T(8,128)S(1)} %div.48) | copy-start | bytes 1966084
  506.1 273.5 %all-gather.37.cloned.1.call-start = ((), (), s32[]{:S(2)}) async-start(), calls=%async_computation.16 | async-start | bytes 2949120 | tf_op jit(solution)/shard_map/all_gather | solution.py:116
  506.7 272.9 %all-gather.39.cloned.1.call-start = ((), (), s32[]{:S(2)}) async-start(), calls=%async_computation.17 | async-start | bytes 2949120 | tf_op jit(solution)/shard_map/all_gather | solution.py:117
  511.1 49.6 %copy-start.27 = (bf16[128,1280]{1,0:T(8,128)(2,1)S(1)}, bf16[128,1280]{1,0:T(8,128)(2,1)}, u32[]{:S(2)}) copy-start(bf16[128,1280]{1,0:T(8,128)(2,1)} %get-tuple-element.314) | copy-start | bytes 983044
  511.1 407.3 %reduce-scatter.7.cloned.1.call-start = ((), (), s32[]{:S(2)}) async-start(), calls=%async_computation.22 | async-start | bytes 6758400 | tf_op jit(solution)/shard_map/reduce_scatter | solution.py:276
  665.5 401.4 %reduce-scatter.13.cloned.1.call-start = ((), (), s32[]{:S(2)}) async-start(), calls=%async_computation.25 | async-start | bytes 6758400 | tf_op jit(solution)/shard_map/reduce_scatter | solution.py:279
  671.6 543.0 %reduce-scatter.15.cloned.1.call-start = ((), (), s32[]{:S(2)}) async-start(), calls=%async_computation.26 | async-start | bytes 6758400 | tf_op jit(solution)/shard_map/reduce_scatter | solution.py:280
  677.6 685.5 %reduce-scatter.17.cloned.1.call-start = ((), (), s32[]{:S(2)}) async-start(), calls=%async_computation.27 | async-start | bytes 6758400 | tf_op jit(solution)/shard_map/reduce_scatter | solution.py:281
  684.7 826.1 %reduce-scatter.9.cloned.1.call-start = ((), (), s32[]{:S(2)}) async-start(), calls=%async_computation.23 | async-start | bytes 6758400 | tf_op jit(solution)/shard_map/reduce_scatter | solution.py:277
  743.8 35.8 %copy-start.19 = (bf16[128,1280]{1,0:T(8,128)(2,1)S(1)}, bf16[128,1280]{1,0:T(8,128)(2,1)}, u32[]{:S(2)}) copy-start(bf16[128,1280]{1,0:T(8,128)(2,1)} %copy-done.18) | copy-start | bytes 983044
  817.5 842.0 %reduce-scatter.11.cloned.1.call-start = ((), (), s32[]{:S(2)}) async-start(), calls=%async_computation.24 | async-start | bytes 6758400 | tf_op jit(solution)/shard_map/reduce_scatter | solution.py:278
  840.5 43.8 %copy-start.13 = (f32[128,1280]{1,0:T(8,128)S(1)}, f32[128,1280]{1,0:T(8,128)}, u32[]{:S(2)}) copy-start(f32[128,1280]{1,0:T(8,128)} %copy-done.11) | copy-start | bytes 1966084
  840.5 43.8 %copy-start.14 = (f32[128,1280]{1,0:T(8,128)S(1)}, f32[128,1280]{1,0:T(8,128)}, u32[]{:S(2)}) copy-start(f32[128,1280]{1,0:T(8,128)} %get-tuple-element.299) | copy-start | bytes 1966084
  (35 other events, 120.6 us)
Sparse Core Ops, SparseCore 0:
  10.9 62.0 all-gather.18
  75.8 58.2 all-gather.16
  137.0 58.2 all-gather.22
  197.4 54.9 all-gather.30
  253.8 54.8 all-gather.20
  311.4 58.1 all-gather.24
  372.4 58.2 all-gather.26
  433.5 58.2 all-gather.28
  493.5 32.7 all-gather.40
  527.8 32.8 all-gather.42
  562.3 32.8 all-gather.32
  596.7 32.8 all-gather.34
  631.3 32.8 all-gather.44
  665.7 33.3 all-gather.46
  700.6 33.5 all-gather.36
  735.7 32.7 all-gather.38
  771.2 147.0 reduce-scatter.6
  921.1 145.7 reduce-scatter.12
  1069.7 144.8 reduce-scatter.14
  1217.4 145.7 reduce-scatter.16
  1366.1 144.7 reduce-scatter.8
  1513.7 145.7 reduce-scatter.10
